TPU v7x, 32 devices: a whole 2x2x4 slice. The times are simulated.
32 devices in a mesh: ctx: 8 (over z, y), head: 4 (over x, core).
Axes of the slice: x: 2, y: 2, z: 4, core: 2. Of those that a mesh axis runs over, the one named last changes fastest.
Arguments:
- queries: bfloat16 [2048, 4096], P(('ctx', 'head')), may hold values from -6 to 6
- key_rows: bfloat16 [2048, 512], P(('ctx', 'head')), may hold values from -6 to 6
- value_rows: bfloat16 [2048, 512], P(('ctx', 'head')), may hold values from -6 to 6
- attn_out: bfloat16 [2048, 4096], P(('ctx', 'head')), may hold values from -6 to 6
- out_grad: bfloat16 [2048, 4096], P(('ctx', 'head')), may hold values from -864 to 864
- logsumexp: float32 [32, 2048], P('head', 'ctx'), may hold values from 7.5 to 8.7
Outputs:
- grad_queries: float32 [2048, 4096], P(('ctx', 'head'))
- grad_keys: float32 [2048, 512], P(('ctx', 'head'))
- grad_values: float32 [2048, 512], P(('ctx', 'head'))
All inputs are finite; a program needn't handle non-finite values.
Results may differ from a plain program's by a relative error of at most 0.0051.
Values may be sent and summed in bfloat16 or wider, within the bound.
No kernel may reach another device: no remote copies, remote signals or barrier semaphores. Data moves between devices by JAX's collectives and lax.ppermute only.
A program may use at most 64 MiB of HBM per device.

v0:
```python
import math
import jax
import jax.numpy as jnp
from jax import lax
from jax.sharding import PartitionSpec as P

HEAD_DIM = 128
GROUP = 8
BLOCK = 256


def from_partner(value, axis, distance):
    return lax.ppermute(value, axis, [(i, i ^ 1 << distance) for i in range(lax.axis_size(axis))])


def block_grads(query_blk, grad_blk, lse_rows, dot_rows, key_blk, value_blk):
    score_scale = 1.0 / math.sqrt(query_blk.shape[-1])
    scores = (
        jnp.einsum("nbhgd,nkhd->nhgbk", query_blk, key_blk, preferred_element_type=jnp.float32)
        * score_scale
    )
    attn_probs = jnp.exp(scores - lse_rows[..., None])
    dprobs = jnp.einsum(
        "nbhgd,nkhd->nhgbk", grad_blk, value_blk, preferred_element_type=jnp.float32
    )
    dscores = (attn_probs * (dprobs - dot_rows[..., None])).astype(jnp.bfloat16)
    weights = attn_probs.astype(jnp.bfloat16)
    d_values = jnp.einsum(
        "nhgbk,nbhgd->nkhd", weights, grad_blk, preferred_element_type=jnp.float32
    )
    d_query = (
        jnp.einsum("nhgbk,nkhd->nbhgd", dscores, key_blk, preferred_element_type=jnp.float32)
        * score_scale
    )
    d_keys = (
        jnp.einsum("nhgbk,nbhgd->nkhd", dscores, query_blk, preferred_element_type=jnp.float32)
        * score_scale
    )
    return (d_query, d_keys, d_values)


def on_device(queries, key_rows, value_rows, attn_out, out_grad, logsumexp):
    rows_before = queries.shape[0]
    dot_before = jnp.sum(
        (out_grad.astype(jnp.float32) * attn_out.astype(jnp.float32)).reshape(
            rows_before, -1, HEAD_DIM
        ),
        axis=2,
    )
    q_local, k_local, v_local, g_local = (
        lax.all_to_all(queries, "head", split_axis=1, concat_axis=0, tiled=True),
        lax.all_to_all(key_rows, "head", split_axis=1, concat_axis=0, tiled=True),
        lax.all_to_all(value_rows, "head", split_axis=1, concat_axis=0, tiled=True),
        lax.all_to_all(out_grad, "head", split_axis=1, concat_axis=0, tiled=True),
    )
    dot_local = lax.all_to_all(dot_before, "head", split_axis=1, concat_axis=0, tiled=True)
    row_count = q_local.shape[0]
    blocks = row_count // BLOCK
    kv_heads = k_local.shape[1] // HEAD_DIM
    query_blk = q_local.reshape(blocks, BLOCK, kv_heads, GROUP, HEAD_DIM)
    grad_blk = g_local.reshape(blocks, BLOCK, kv_heads, GROUP, HEAD_DIM)
    key_blk = k_local.reshape(blocks, BLOCK, kv_heads, HEAD_DIM)
    value_blk = v_local.reshape(blocks, BLOCK, kv_heads, HEAD_DIM)
    lse_rows = logsumexp.reshape(kv_heads, GROUP, blocks, BLOCK).transpose(2, 0, 1, 3)
    dot_rows = dot_local.reshape(blocks, BLOCK, kv_heads, GROUP).transpose(0, 2, 3, 1)
    grad_q, grad_k, grad_v = block_grads(
        query_blk, grad_blk, lse_rows, dot_rows, key_blk, value_blk
    )
    ctx_levels = lax.axis_size("ctx").bit_length() - 1
    plan = list(range(ctx_levels))
    for bit_level in plan:
        far_k, far_v = from_partner((key_blk, value_blk), "ctx", bit_level)
        part_q, part_k, part_v = block_grads(query_blk, grad_blk, lse_rows, dot_rows, far_k, far_v)
        back_k, back_v = from_partner((part_k, part_v), "ctx", bit_level)
        grad_q = grad_q + part_q
        grad_k = grad_k + back_k
        grad_v = grad_v + back_v
    result_q, result_k, result_v = (
        lax.all_to_all(
            grad_q.reshape(row_count, -1), "head", split_axis=0, concat_axis=1, tiled=True
        ),
        lax.all_to_all(
            grad_k.reshape(row_count, -1), "head", split_axis=0, concat_axis=1, tiled=True
        ),
        lax.all_to_all(
            grad_v.reshape(row_count, -1), "head", split_axis=0, concat_axis=1, tiled=True
        ),
    )
    return (result_q, result_k, result_v)


def solution(mesh):
    placed = (
        P(("ctx", "head"), None),
        P(("ctx", "head"), None),
        P(("ctx", "head"), None),
        P(("ctx", "head"), None),
        P(("ctx", "head"), None),
        P("head", "ctx"),
    )
    return jax.shard_map(
        on_device,
        mesh=mesh,
        in_specs=placed,
        out_specs=(P(("ctx", "head"), None), P(("ctx", "head"), None), P(("ctx", "head"), None)),
        check_vma=False,
    )
```

profile of v0, /device:TPU:0, one launch (start us, length us, event | category | flops | bytes accessed | tf_op | source)
XLA Modules:
  0.0 108.8 jit_solution(2686458098232040991)
XLA Ops:
  0.6 1.3 %multiply_bitcast_fusion = f32[8,8,32,128]{3,1,2,0:T(8,128)S(1)} fusion(bf16[64,4096]{1,0:T(8,128)(2,1)} %param.9, bf16[64,4096]{1,0:T(8,128)(2,1)} %param.10), kind=kLoop, calls=%fused_computation.59 | loop fusion | flops 786432 | bytes 2097152
  2.0 0.2 copy.116
  2.2 0.3 reduce_sum.9
  2.6 0.7 reshape.241
  3.3 4.2 %all-to-all-start.4 = ((f32[4,1,512]{2,1,0:T(1,128)}), f32[4,1,512]{2,1,0:T(1,128)S(1)}, u32[]{:S(2)}, u32[]{:S(2)}) async-start(f32[4,1,512]{2,1,0:T(1,128)} %reshape.241), calls=%async_computation.4 | async-start | bytes 16384 | tf_op jit(solution)/shard_map/all_to_all | solution.py:56
  7.6 0.6 copy_bitcast_fusion.5
  8.2 3.2 %all-to-all-done.4 = f32[4,1,512]{2,1,0:T(1,128)S(1)} async-done(((f32[4,1,512]{2,1,0:T(1,128)}), f32[4,1,512]{2,1,0:T(1,128)S(1)}, u32[]{:S(2)}, u32[]{:S(2)}) %all-to-all-start.4) | async-done | bytes 8224 | tf_op jit(solution)/shard_map/all_to_all | solution.py:56
  11.4 3.3 %all-to-all-start = ((bf16[64,4,128]{2,0,1:T(8,128)(2,1)}), bf16[64,4,128]{2,0,1:T(8,128)(2,1)S(1)}, u32[]{:S(2)}, u32[]{:S(2)}) async-start(bf16[64,4,128]{2,0,1:T(8,128)(2,1)} %copy_bitcast_fusion.5), calls=%async_computation | async-start | bytes 131072 | tf_op jit(solution)/shard_map/all_to_all | solution.py:52
  14.7 0.6 copy_bitcast_fusion.4
  15.3 3.4 %all-to-all-done = bf16[64,4,128]{2,0,1:T(8,128)(2,1)S(1)} async-done(((bf16[64,4,128]{2,0,1:T(8,128)(2,1)}), bf16[64,4,128]{2,0,1:T(8,128)(2,1)S(1)}, u32[]{:S(2)}, u32[]{:S(2)}) %all-to-all-start) | async-done | bytes 65568 | tf_op jit(solution)/shard_map/all_to_all | solution.py:52
  18.8 3.3 %all-to-all-start.2 = ((bf16[64,4,128]{2,0,1:T(8,128)(2,1)}), bf16[64,4,128]{2,0,1:T(8,128)(2,1)S(1)}, u32[]{:S(2)}, u32[]{:S(2)}) async-start(bf16[64,4,128]{2,0,1:T(8,128)(2,1)} %copy_bitcast_fusion.4), calls=%async_computation.2 | async-start | bytes 131072 | tf_op jit(solution)/shard_map/all_to_all | solution.py:53
  22.1 0.8 copy.156
  22.9 3.2 %all-to-all-done.2 = bf16[64,4,128]{2,0,1:T(8,128)(2,1)S(1)} async-done(((bf16[64,4,128]{2,0,1:T(8,128)(2,1)}), bf16[64,4,128]{2,0,1:T(8,128)(2,1)S(1)}, u32[]{:S(2)}, u32[]{:S(2)}) %all-to-all-start.2) | async-done | bytes 65568 | tf_op jit(solution)/shard_map/all_to_all | solution.py:53
  26.1 3.5 %all-to-all-start.1 = ((bf16[64,4,1024]{2,0,1:T(8,128)(2,1)}), bf16[64,4,1024]{2,0,1:T(8,128)(2,1)S(1)}, u32[]{:S(2)}, u32[]{:S(2)}) async-start(bf16[64,4,1024]{2,0,1:T(8,128)(2,1)} %bitcast.347), calls=%async_computation.1 | async-start | bytes 1048576 | tf_op jit(solution)/shard_map/all_to_all | solution.py:51
  29.6 0.9 copy.155
  30.5 7.9 %all-to-all-done.1 = bf16[64,4,1024]{2,0,1:T(8,128)(2,1)S(1)} async-done(((bf16[64,4,1024]{2,0,1:T(8,128)(2,1)}), bf16[64,4,1024]{2,0,1:T(8,128)(2,1)S(1)}, u32[]{:S(2)}, u32[]{:S(2)}) %all-to-all-start.1) | async-done | bytes 524320 | tf_op jit(solution)/shard_map/all_to_all | solution.py:51
  38.4 3.5 %all-to-all-start.3 = ((bf16[64,4,1024]{2,0,1:T(8,128)(2,1)}), bf16[64,4,1024]{2,0,1:T(8,128)(2,1)S(1)}, u32[]{:S(2)}, u32[]{:S(2)}) async-start(bf16[64,4,1024]{2,0,1:T(8,128)(2,1)} %bitcast.346), calls=%async_computation.3 | async-start | bytes 1048576 | tf_op jit(solution)/shard_map/all_to_all | solution.py:54
  41.9 0.5 broadcast.95
  42.4 0.7 reduce
  43.1 2.0 %collective-permute-start = (bf16[1,256,1,128]{3,1,2,0:T(8,128)(2,1)S(1)}, bf16[1,256,1,128]{3,1,2,0:T(8,128)(2,1)S(1)}, u32[]{:S(2)}, u32[]{:S(2)}) collective-permute-start(bf16[1,256,1,128]{3,1,2,0:T(8,128)(2,1)S(1)} %bitcast.370), channel_id=1, source_target_pairs={{0,4},{4,0},{8,12},{12,8},{16,20},{20,16},{24,28},{28,24},{1,5},{5... | collective-permute-start | bytes 196616 | tf_op jit(solution)/shard_map/ppermute | solution.py:13
  45.2 2.6 %collective-permute-start.5 = (bf16[1,256,1,128]{3,1,2,0:T(8,128)(2,1)S(1)}, bf16[1,256,1,128]{3,1,2,0:T(8,128)(2,1)S(1)}, u32[]{:S(2)}, u32[]{:S(2)}) collective-permute-start(bf16[1,256,1,128]{3,1,2,0:T(8,128)(2,1)S(1)} %bitcast.376), channel_id=1, source_target_pairs={{0,16},{4,20},{8,24},{12,28},{16,0},{20,4},{24,8},{28,12},{1,17},{... | collective-permute-start | bytes 196616 | tf_op jit(solution)/shard_map/ppermute | solution.py:13
  47.8 1.6 %collective-permute-start.3 = (bf16[1,256,1,128]{3,1,2,0:T(8,128)(2,1)S(1)}, bf16[1,256,1,128]{3,1,2,0:T(8,128)(2,1)S(1)}, u32[]{:S(2)}, u32[]{:S(2)}) collective-permute-start(bf16[1,256,1,128]{3,1,2,0:T(8,128)(2,1)S(1)} %bitcast.377), channel_id=1, source_target_pairs={{0,8},{4,12},{8,0},{12,4},{16,24},{20,28},{24,16},{28,20},{1,9},{5... | collective-permute-start | bytes 196616 | tf_op jit(solution)/shard_map/ppermute | solution.py:13
  49.4 0.5 collective-permute-start.1
  49.9 0.3 collective-permute-start.4
  50.4 0.3 all-to-all-done.3
  50.8 2.1 %collective-permute-start.2 = (bf16[1,256,1,128]{3,1,2,0:T(8,128)(2,1)S(1)}, bf16[1,256,1,128]{3,1,2,0:T(8,128)(2,1)S(1)}, u32[]{:S(2)}, u32[]{:S(2)}) collective-permute-start(bf16[1,256,1,128]{3,1,2,0:T(8,128)(2,1)S(1)} %bitcast.372), channel_id=1, source_target_pairs={{0,8},{4,12},{8,0},{12,4},{16,24},{20,28},{24,16},{28,20},{1,9},{5... | collective-permute-start | bytes 196616 | tf_op jit(solution)/shard_map/ppermute | solution.py:13
  52.9 0.4 fusion.69
  53.3 0.6 convolution_bitcast_fusion.2
  53.9 0.6 fusion.17
  54.5 0.4 fusion.28
  55.0 1.6 %collective-permute-start.6 = (f32[1,256,1,128]{3,1,2,0:T(8,128)S(1)}, f32[1,256,1,128]{3,1,2,0:T(8,128)S(1)}, u32[]{:S(2)}, u32[]{:S(2)}) collective-permute-start(f32[1,256,1,128]{3,1,2,0:T(8,128)S(1)} %fusion.28), channel_id=1, source_target_pairs={{0,4},{4,0},{8,12},{12,8},{16,20},{20,16},{24,28},{28,24},{1,5},{5... | collective-permute-start | bytes 393224 | tf_op jit(solution)/shard_map/ppermute | solution.py:13
  56.5 0.4 fusion.67
  57.0 0.6 fusion.18
  57.6 1.1 fusion.26
  58.7 0.6 collective-permute-start.7
  59.3 0.4 fusion.71
  59.7 0.6 fusion.16
  60.4 0.5 fusion.87
  60.9 0.6 convolution_bitcast_fusion.1
  61.4 1.6 %collective-permute-start.9 = (f32[1,256,1,128]{3,1,2,0:T(8,128)S(1)}, f32[1,256,1,128]{3,1,2,0:T(8,128)S(1)}, u32[]{:S(2)}, u32[]{:S(2)}) collective-permute-start(f32[1,256,1,128]{3,1,2,0:T(8,128)S(1)} %convolution_bitcast_fusion.2), channel_id=1, source_target_pairs={{0,4},{4,0},{8,12},{12,8},{16,20},{20,16},{24,28},{28,24},{1,5},{5... | collective-permute-start | bytes 393224 | tf_op jit(solution)/shard_map/ppermute | solution.py:13
  63.0 1.1 %collective-permute-start.10 = (f32[1,256,1,128]{3,1,2,0:T(8,128)S(1)}, f32[1,256,1,128]{3,1,2,0:T(8,128)S(1)}, u32[]{:S(2)}, u32[]{:S(2)}) collective-permute-start(f32[1,256,1,128]{3,1,2,0:T(8,128)S(1)} %convolution_bitcast_fusion.1), channel_id=1, source_target_pairs={{0,8},{4,12},{8,0},{12,4},{16,24},{20,28},{24,16},{28,20},{1,9},{5... | collective-permute-start | bytes 393224 | tf_op jit(solution)/shard_map/ppermute | solution.py:13
  64.1 0.4 fusion.65
  64.5 0.6 convolution_bitcast_fusion
  65.1 2.0 %collective-permute-start.11 = (f32[1,256,1,128]{3,1,2,0:T(8,128)S(1)}, f32[1,256,1,128]{3,1,2,0:T(8,128)S(1)}, u32[]{:S(2)}, u32[]{:S(2)}) collective-permute-start(f32[1,256,1,128]{3,1,2,0:T(8,128)S(1)} %convolution_bitcast_fusion), channel_id=1, source_target_pairs={{0,16},{4,20},{8,24},{12,28},{16,0},{20,4},{24,8},{28,12},{1,17},{... | collective-permute-start | bytes 393224 | tf_op jit(solution)/shard_map/ppermute | solution.py:13
  67.1 0.6 fusion.19
  67.7 1.5 %fusion.74 = f32[8,256,128]{2,1,0:T(8,128)} fusion(bf16[8,256,256]{1,2,0:T(8,128)(2,1)S(1)} %fusion.19, bf16[1,256,1,128]{3,1,2,0:T(8,128)(2,1)S(1)} %collective-permute-done.4), kind=kOutput, calls=%fused_computation.95 | convolution fusion | flops 134217728 | bytes 2162688 | tf_op jit(solution)/shard_map/nhgbk,nkhd->nbhgd/dot_general | solution.py:32
  69.2 1.5 %convolution_add_fusion.1 = f32[8,256,128]{2,1,0:T(8,128)} fusion(f32[8,256,128]{2,1,0:T(8,128)S(1)} %fusion.87, bf16[8,256,256]{1,2,0:T(8,128)(2,1)S(1)} %fusion.17, bf16[1,256,1,128]{3,1,2,0:T(8,128)(2,1)S(1)} %collective-permute-done), kind=kOutput, calls=%fused_computation.30 | convolution fusion | flops 134479872 | bytes 3211264 | tf_op jit(solution)/shard_map/nhgbk,nkhd->nbhgd/dot_general | solution.py:32
  70.7 1.1 fusion.24
  71.8 1.0 collective-permute-start.8
  72.8 1.2 %fusion.36 = f32[1,256,1,128]{3,1,2,0:T(8,128)} fusion(f32[1,256,1,128]{3,1,2,0:T(8,128)S(1)} %collective-permute-done.11, f32[1,256,1,128]{3,1,2,0:T(8,128)S(1)} %collective-permute-done.10, f32[1,256,1,128]{3,1,2,0:T(8,128)S(1)} %collective-permute-done.9, f32[256,256,8]{1,0,2:T(8,128)S(1)} %fusion.71, f32[8,256]{1,0:T(8,128)S(1)} %copy-done.2, ...), kind=kOutput, calls=%fused_computation.54 | convolution fusion | flops 135888896 | bytes 3153920 | tf_op jit(solution)/shard_map/nhgbk,nbhgd->nkhd/dot_general | solution.py:28
  74.0 3.3 %all-to-all-start.7 = ((f32[4,64,128]{2,1,0:T(8,128)}), f32[4,64,128]{2,1,0:T(8,128)S(1)}, u32[]{:S(2)}, u32[]{:S(2)}) async-start(f32[4,64,128]{2,1,0:T(8,128)} %bitcast.90), calls=%async_computation.7 | async-start | bytes 262144 | tf_op jit(solution)/shard_map/all_to_all | solution.py:85
  77.4 1.9 %collective-permute-done.8 = f32[1,256,1,128]{3,1,2,0:T(8,128)S(1)} collective-permute-done((f32[1,256,1,128]{3,1,2,0:T(8,128)}, f32[1,256,1,128]{3,1,2,0:T(8,128)S(1)}, u32[]{:S(2)}, u32[]{:S(2)}) %collective-permute-start.8) | collective-permute-done | bytes 131104 | tf_op jit(solution)/shard_map/ppermute | solution.py:13
  79.3 1.1 %fusion.33 = f32[1,256,1,128]{3,1,2,0:T(8,128)} fusion(f32[1,256,1,128]{3,1,2,0:T(8,128)S(1)} %collective-permute-done.8, f32[1,256,1,128]{3,1,2,0:T(8,128)S(1)} %collective-permute-done.7, f32[1,256,1,128]{3,1,2,0:T(8,128)S(1)} %collective-permute-done.6, bf16[8,256,256]{1,2,0:T(8,128)(2,1)S(1)} %fusion.16, bf16[256,8,128]{2,1,0:T(8,128)(2,1)S(1)} %bitcast.363), kind=kOutput, calls=%fused_computation.51 | convolution fusion | flops 134348800 | bytes 2097152 | tf_op jit(solution)/shard_map/nhgbk,nbhgd->nkhd/dot_general | solution.py:36
  80.4 1.6 %all-to-all-done.7 = f32[4,64,128]{2,1,0:T(8,128)S(1)} async-done(((f32[4,64,128]{2,1,0:T(8,128)}), f32[4,64,128]{2,1,0:T(8,128)S(1)}, u32[]{:S(2)}, u32[]{:S(2)}) %all-to-all-start.7) | async-done | bytes 131104 | tf_op jit(solution)/shard_map/all_to_all | solution.py:85
  81.9 3.3 %all-to-all-start.6 = ((f32[4,64,128]{2,1,0:T(8,128)}), f32[4,64,128]{2,1,0:T(8,128)S(1)}, u32[]{:S(2)}, u32[]{:S(2)}) async-start(f32[4,64,128]{2,1,0:T(8,128)} %bitcast.68), calls=%async_computation.6 | async-start | bytes 262144 | tf_op jit(solution)/shard_map/all_to_all | solution.py:82
  85.3 2.0 %fusion.22 = f32[1,256,1,8,128]{4,1,3,2,0:T(8,128)S(1)} fusion(f32[8,256,128]{2,1,0:T(8,128)} %fusion.74, f32[8,256,128]{2,1,0:T(8,128)} %convolution_add_fusion.1, bf16[8,256,256]{1,2,0:T(8,128)(2,1)S(1)} %fusion.18, bf16[1,256,1,128]{3,1,2,0:T(8,128)(2,1)S(1)} %collective-permute-done.2), kind=kOutput, calls=%fused_computation.32 | convolution fusion | flops 135004160 | bytes 4259840 | tf_op jit(solution)/shard_map/nhgbk,nkhd->nbhgd/dot_general | solution.py:32
  87.3 0.6 copy.91
  87.9 1.1 %all_to_all.117 = f32[4,64,1024]{2,1,0:T(8,128)} reshape(f32[1,256,1,8,128]{4,3,1,2,0:T(8,128)S(1)} %copy.91) | data formatting | bytes 2097152 | tf_op jit(solution)/shard_map/all_to_all | solution.py:79
  89.0 0.8 all-to-all-done.6
  89.8 3.5 %all-to-all-start.5 = ((f32[4,64,1024]{2,1,0:T(8,128)}), f32[4,64,1024]{2,1,0:T(8,128)S(1)}, u32[]{:S(2)}, u32[]{:S(2)}) async-start(f32[4,64,1024]{2,1,0:T(8,128)} %all_to_all.117), calls=%async_computation.5 | async-start | bytes 2097152 | tf_op jit(solution)/shard_map/all_to_all | solution.py:79
  93.4 0.7 copy_bitcast_fusion.2
  94.0 0.7 copy_bitcast_fusion.3
  94.7 13.1 %all-to-all-done.5 = f32[4,64,1024]{2,1,0:T(8,128)S(1)} async-done(((f32[4,64,1024]{2,1,0:T(8,128)}), f32[4,64,1024]{2,1,0:T(8,128)S(1)}, u32[]{:S(2)}, u32[]{:S(2)}) %all-to-all-start.5) | async-done | bytes 1048608 | tf_op jit(solution)/shard_map/all_to_all | solution.py:79
  107.8 1.0 copy.111
  (29 shorter events, 0.5 us)
Async XLA Ops:
  0.6 6.9 %copy-start = (bf16[64,512]{1,0:T(8,128)(2,1)S(1)}, bf16[64,512]{1,0:T(8,128)(2,1)}, u32[]{:S(2)}) copy-start(bf16[64,512]{1,0:T(8,128)(2,1)} %param.7) | copy-start | bytes 196612
  2.0 12.7 %copy-start.4 = (bf16[64,512]{1,0:T(8,128)(2,1)S(1)}, bf16[64,512]{1,0:T(8,128)(2,1)}, u32[]{:S(2)}) copy-start(bf16[64,512]{1,0:T(8,128)(2,1)} %param.8) | copy-start | bytes 196612
  2.0 20.1 %copy-start.3 = (bf16[64,4096]{1,0:T(8,128)(2,1)S(1)}, bf16[64,4096]{1,0:T(8,128)(2,1)}, u32[]{:S(2)}) copy-start(bf16[64,4096]{1,0:T(8,128)(2,1)} %param.6) | copy-start | bytes 1572868
  2.2 27.4 %copy-start.1 = (bf16[64,4096]{1,0:T(8,128)(2,1)S(1)}, bf16[64,4096]{1,0:T(8,128)(2,1)}, u32[]{:S(2)}) copy-start(bf16[64,4096]{1,0:T(8,128)(2,1)} %param.10) | copy-start | bytes 1572868
  3.3 8.1 %all-to-all-start.4 = ((f32[4,1,512]{2,1,0:T(1,128)}), f32[4,1,512]{2,1,0:T(1,128)S(1)}, u32[]{:S(2)}, u32[]{:S(2)}) async-start(f32[4,1,512]{2,1,0:T(1,128)} %reshape.241), calls=%async_computation.4 | async-start | bytes 16384 | tf_op jit(solution)/shard_map/all_to_all | solution.py:56
  11.4 7.4 %all-to-all-start = ((bf16[64,4,128]{2,0,1:T(8,128)(2,1)}), bf16[64,4,128]{2,0,1:T(8,128)(2,1)S(1)}, u32[]{:S(2)}, u32[]{:S(2)}) async-start(bf16[64,4,128]{2,0,1:T(8,128)(2,1)} %copy_bitcast_fusion.5), calls=%async_computation | async-start | bytes 131072 | tf_op jit(solution)/shard_map/all_to_all | solution.py:52
  18.8 7.4 %all-to-all-start.2 = ((bf16[64,4,128]{2,0,1:T(8,128)(2,1)}), bf16[64,4,128]{2,0,1:T(8,128)(2,1)S(1)}, u32[]{:S(2)}, u32[]{:S(2)}) async-start(bf16[64,4,128]{2,0,1:T(8,128)(2,1)} %copy_bitcast_fusion.4), calls=%async_computation.2 | async-start | bytes 131072 | tf_op jit(solution)/shard_map/all_to_all | solution.py:53
  26.1 12.3 %all-to-all-start.1 = ((bf16[64,4,1024]{2,0,1:T(8,128)(2,1)}), bf16[64,4,1024]{2,0,1:T(8,128)(2,1)S(1)}, u32[]{:S(2)}, u32[]{:S(2)}) async-start(bf16[64,4,1024]{2,0,1:T(8,128)(2,1)} %bitcast.347), calls=%async_computation.1 | async-start | bytes 1048576 | tf_op jit(solution)/shard_map/all_to_all | solution.py:51
  38.4 12.3 %all-to-all-start.3 = ((bf16[64,4,1024]{2,0,1:T(8,128)(2,1)}), bf16[64,4,1024]{2,0,1:T(8,128)(2,1)S(1)}, u32[]{:S(2)}, u32[]{:S(2)}) async-start(bf16[64,4,1024]{2,0,1:T(8,128)(2,1)} %bitcast.346), calls=%async_computation.3 | async-start | bytes 1048576 | tf_op jit(solution)/shard_map/all_to_all | solution.py:54
  43.1 7.6 %collective-permute-start = (bf16[1,256,1,128]{3,1,2,0:T(8,128)(2,1)S(1)}, bf16[1,256,1,128]{3,1,2,0:T(8,128)(2,1)S(1)}, u32[]{:S(2)}, u32[]{:S(2)}) collective-permute-start(bf16[1,256,1,128]{3,1,2,0:T(8,128)(2,1)S(1)} %bitcast.370), channel_id=1, source_target_pairs={{0,4},{4,0},{8,12},{12,8},{16,20},{20,16},{24,28},{28,24},{1,5},{5... | collective-permute-start | bytes 196616 | tf_op jit(solution)/shard_map/ppermute | solution.py:13
  45.2 19.9 %collective-permute-start.5 = (bf16[1,256,1,128]{3,1,2,0:T(8,128)(2,1)S(1)}, bf16[1,256,1,128]{3,1,2,0:T(8,128)(2,1)S(1)}, u32[]{:S(2)}, u32[]{:S(2)}) collective-permute-start(bf16[1,256,1,128]{3,1,2,0:T(8,128)(2,1)S(1)} %bitcast.376), channel_id=1, source_target_pairs={{0,16},{4,20},{8,24},{12,28},{16,0},{20,4},{24,8},{28,12},{1,17},{... | collective-permute-start | bytes 196616 | tf_op jit(solution)/shard_map/ppermute | solution.py:13
  47.8 9.2 %collective-permute-start.3 = (bf16[1,256,1,128]{3,1,2,0:T(8,128)(2,1)S(1)}, bf16[1,256,1,128]{3,1,2,0:T(8,128)(2,1)S(1)}, u32[]{:S(2)}, u32[]{:S(2)}) collective-permute-start(bf16[1,256,1,128]{3,1,2,0:T(8,128)(2,1)S(1)} %bitcast.377), channel_id=1, source_target_pairs={{0,8},{4,12},{8,0},{12,4},{16,24},{20,28},{24,16},{28,20},{1,9},{5... | collective-permute-start | bytes 196616 | tf_op jit(solution)/shard_map/ppermute | solution.py:13
  49.4 4.5 %collective-permute-start.1 = (bf16[1,256,1,128]{3,1,2,0:T(8,128)(2,1)S(1)}, bf16[1,256,1,128]{3,1,2,0:T(8,128)(2,1)S(1)}, u32[]{:S(2)}, u32[]{:S(2)}) collective-permute-start(bf16[1,256,1,128]{3,1,2,0:T(8,128)(2,1)S(1)} %bitcast.378), channel_id=1, source_target_pairs={{0,4},{4,0},{8,12},{12,8},{16,20},{20,16},{24,28},{28,24},{1,5},{5... | collective-permute-start | bytes 196616 | tf_op jit(solution)/shard_map/ppermute | solution.py:13
  49.9 13.1 %collective-permute-start.4 = (bf16[1,256,1,128]{3,1,2,0:T(8,128)(2,1)S(1)}, bf16[1,256,1,128]{3,1,2,0:T(8,128)(2,1)S(1)}, u32[]{:S(2)}, u32[]{:S(2)}) collective-permute-start(bf16[1,256,1,128]{3,1,2,0:T(8,128)(2,1)S(1)} %bitcast.371), channel_id=1, source_target_pairs={{0,16},{4,20},{8,24},{12,28},{16,0},{20,4},{24,8},{28,12},{1,17},{... | collective-permute-start | bytes 196616 | tf_op jit(solution)/shard_map/ppermute | solution.py:13
  50.3 3.0 %copy-start.2 = (f32[8,256]{1,0:T(8,128)S(1)}, f32[8,256]{1,0:T(8,128)}, u32[]{:S(2)}) copy-start(f32[8,256]{1,0:T(8,128)} %param.11) | copy-start | bytes 24580
  50.8 5.8 %collective-permute-start.2 = (bf16[1,256,1,128]{3,1,2,0:T(8,128)(2,1)S(1)}, bf16[1,256,1,128]{3,1,2,0:T(8,128)(2,1)S(1)}, u32[]{:S(2)}, u32[]{:S(2)}) collective-permute-start(bf16[1,256,1,128]{3,1,2,0:T(8,128)(2,1)S(1)} %bitcast.372), channel_id=1, source_target_pairs={{0,8},{4,12},{8,0},{12,4},{16,24},{20,28},{24,16},{28,20},{1,9},{5... | collective-permute-start | bytes 196616 | tf_op jit(solution)/shard_map/ppermute | solution.py:13
  55.0 22.4 %collective-permute-start.6 = (f32[1,256,1,128]{3,1,2,0:T(8,128)S(1)}, f32[1,256,1,128]{3,1,2,0:T(8,128)S(1)}, u32[]{:S(2)}, u32[]{:S(2)}) collective-permute-start(f32[1,256,1,128]{3,1,2,0:T(8,128)S(1)} %fusion.28), channel_id=1, source_target_pairs={{0,4},{4,0},{8,12},{12,8},{16,20},{20,16},{24,28},{28,24},{1,5},{5... | collective-permute-start | bytes 393224 | tf_op jit(solution)/shard_map/ppermute | solution.py:13
  58.7 18.7 %collective-permute-start.7 = (f32[1,256,1,128]{3,1,2,0:T(8,128)}, f32[1,256,1,128]{3,1,2,0:T(8,128)S(1)}, u32[]{:S(2)}, u32[]{:S(2)}) collective-permute-start(f32[1,256,1,128]{3,1,2,0:T(8,128)} %fusion.26), channel_id=1, source_target_pairs={{0,8},{4,12},{8,0},{12,4},{16,24},{20,28},{24,16},{28,20},{1,9},{5... | collective-permute-start | bytes 393224 | tf_op jit(solution)/shard_map/ppermute | solution.py:13
  61.4 10.4 %collective-permute-start.9 = (f32[1,256,1,128]{3,1,2,0:T(8,128)S(1)}, f32[1,256,1,128]{3,1,2,0:T(8,128)S(1)}, u32[]{:S(2)}, u32[]{:S(2)}) collective-permute-start(f32[1,256,1,128]{3,1,2,0:T(8,128)S(1)} %convolution_bitcast_fusion.2), channel_id=1, source_target_pairs={{0,4},{4,0},{8,12},{12,8},{16,20},{20,16},{24,28},{28,24},{1,5},{5... | collective-permute-start | bytes 393224 | tf_op jit(solution)/shard_map/ppermute | solution.py:13
  63.0 9.8 %collective-permute-start.10 = (f32[1,256,1,128]{3,1,2,0:T(8,128)S(1)}, f32[1,256,1,128]{3,1,2,0:T(8,128)S(1)}, u32[]{:S(2)}, u32[]{:S(2)}) collective-permute-start(f32[1,256,1,128]{3,1,2,0:T(8,128)S(1)} %convolution_bitcast_fusion.1), channel_id=1, source_target_pairs={{0,8},{4,12},{8,0},{12,4},{16,24},{20,28},{24,16},{28,20},{1,9},{5... | collective-permute-start | bytes 393224 | tf_op jit(solution)/shard_map/ppermute | solution.py:13
  65.1 7.7 %collective-permute-start.11 = (f32[1,256,1,128]{3,1,2,0:T(8,128)S(1)}, f32[1,256,1,128]{3,1,2,0:T(8,128)S(1)}, u32[]{:S(2)}, u32[]{:S(2)}) collective-permute-start(f32[1,256,1,128]{3,1,2,0:T(8,128)S(1)} %convolution_bitcast_fusion), channel_id=1, source_target_pairs={{0,16},{4,20},{8,24},{12,28},{16,0},{20,4},{24,8},{28,12},{1,17},{... | collective-permute-start | bytes 393224 | tf_op jit(solution)/shard_map/ppermute | solution.py:13
  71.8 7.5 %collective-permute-start.8 = (f32[1,256,1,128]{3,1,2,0:T(8,128)}, f32[1,256,1,128]{3,1,2,0:T(8,128)S(1)}, u32[]{:S(2)}, u32[]{:S(2)}) collective-permute-start(f32[1,256,1,128]{3,1,2,0:T(8,128)} %fusion.24), channel_id=1, source_target_pairs={{0,16},{4,20},{8,24},{12,28},{16,0},{20,4},{24,8},{28,12},{1,17},{... | collective-permute-start | bytes 393224 | tf_op jit(solution)/shard_map/ppermute | solution.py:13
  74.0 7.9 %all-to-all-start.7 = ((f32[4,64,128]{2,1,0:T(8,128)}), f32[4,64,128]{2,1,0:T(8,128)S(1)}, u32[]{:S(2)}, u32[]{:S(2)}) async-start(f32[4,64,128]{2,1,0:T(8,128)} %bitcast.90), calls=%async_computation.7 | async-start | bytes 262144 | tf_op jit(solution)/shard_map/all_to_all | solution.py:85
  81.9 7.9 %all-to-all-start.6 = ((f32[4,64,128]{2,1,0:T(8,128)}), f32[4,64,128]{2,1,0:T(8,128)S(1)}, u32[]{:S(2)}, u32[]{:S(2)}) async-start(f32[4,64,128]{2,1,0:T(8,128)} %bitcast.68), calls=%async_computation.6 | async-start | bytes 262144 | tf_op jit(solution)/shard_map/all_to_all | solution.py:82
  89.8 17.9 %all-to-all-start.5 = ((f32[4,64,1024]{2,1,0:T(8,128)}), f32[4,64,1024]{2,1,0:T(8,128)S(1)}, u32[]{:S(2)}, u32[]{:S(2)}) async-start(f32[4,64,1024]{2,1,0:T(8,128)} %all_to_all.117), calls=%async_computation.5 | async-start | bytes 2097152 | tf_op jit(solution)/shard_map/all_to_all | solution.py:79
where the time goes:
time: 110 us; the launch traced here: 109 us
  starting transfers between devices  44.9 us (41%)
  waiting for transfers between devices  35.4 us (32%)
  matrix products  16.3 us (15%)
  local copies, waits for them, and re-layouts  8.94 us (8%)
  other arithmetic  2.35 us (2%)
    ppermute x12, starting transfers between devices, from_partner(): lax.ppermute(value, axis, [(i, i ^ 1 << distance) for i in range(lax.axis...  17 us
    all_to_all x1, waiting for transfers between devices, on_device(): lax.all_to_all(grad_q.reshape(row_count, -1), 'head', split_axis=0, conca...  13.1 us
    all_to_all x1, waiting for transfers between devices, on_device(): lax.all_to_all(queries, 'head', split_axis=1, concat_axis=0, tiled=True)  7.92 us
    dot_general x4, matrix products, block_grads(): jnp.einsum('nhgbk,nkhd->nbhgd', dscores, key_blk, preferred_element_type=...  5.48 us
    all_to_all x1, starting transfers between devices, on_device(): lax.all_to_all(dot_before, 'head', split_axis=1, concat_axis=0, tiled=True)  4.24 us
    dot_general x4, matrix products, block_grads(): jnp.einsum('nhgbk,nbhgd->nkhd', dscores, query_blk, preferred_element_typ...  3.69 us
    all_to_all x1, starting transfers between devices, on_device(): lax.all_to_all(grad_q.reshape(row_count, -1), 'head', split_axis=0, conca...  3.52 us
    all_to_all x1, starting transfers between devices, on_device(): lax.all_to_all(queries, 'head', split_axis=1, concat_axis=0, tiled=True)  3.47 us
  transfers between devices with their start and end apart: 20, of which 9 were waited for; matrix products, arithmetic and copies ran while one was open for 21% of the time, Pallas kernels for 0%

commit v1 on v0

--- a/solution.py
+++ b/solution.py
@@ -7,6 +7,33 @@
 HEAD_DIM = 128
 GROUP = 8
 BLOCK = 256
+
+
+def build_series_all(tile_in, join_dim, panel):
+    high, local_now = (tile_in.shape[:join_dim], tile_in.shape[join_dim + 1 :])
+    y_new = tile_in.reshape(*high, panel, -1, *local_now)
+    return jnp.moveaxis(y_new, join_dim, 0)
+
+
+def build_the_domain(patch, at_axis):
+    s_next = list(patch.shape[1:])
+    s_next[at_axis] *= patch.shape[0]
+    return jnp.moveaxis(patch, 0, at_axis).reshape(s_next)
+
+
+def refer_the_ratios(chunk, across, values, arr_in=0):
+    n_now = lax.axis_index(across)
+    upper = lax.axis_size(across)
+    now, moved = (upper, n_now)
+    field_out = build_series_all(chunk, values, now)
+    kept_rows = [field_out[moved]]
+    for ii in range(1, now):
+        current_arr = field_out[moved ^ ii]
+        main = lax.ppermute(current_arr, across, [(tick, tick ^ ii) for tick in range(now)])
+        kept_rows.append(main)
+    val2 = jnp.stack(kept_rows, 0)
+    field_out = val2[moved ^ jnp.arange(now)]
+    return build_the_domain(field_out, arr_in)
 
 
 def from_partner(value, axis, distance):
@@ -49,7 +76,7 @@
     )
     q_local, k_local, v_local, g_local = (
         lax.all_to_all(queries, "head", split_axis=1, concat_axis=0, tiled=True),
-        lax.all_to_all(key_rows, "head", split_axis=1, concat_axis=0, tiled=True),
+        refer_the_ratios(key_rows, "head", 1),
         lax.all_to_all(value_rows, "head", split_axis=1, concat_axis=0, tiled=True),
         lax.all_to_all(out_grad, "head", split_axis=1, concat_axis=0, tiled=True),
     )

time: 110 us -> 105 us (0.955)
  the two profiles are of different devices: /device:TPU:0 before, /device:TPU:24 now
where the time goes in v1:
time: 105 us
  starting transfers between devices  41.2 us (39%)
  waiting for transfers between devices  35.7 us (34%)
  matrix products  15.6 us (15%)
  local copies, waits for them, and re-layouts  8.84 us (8%)
  other arithmetic  2.38 us (2%)
    ppermute x12, starting transfers between devices, from_partner(): lax.ppermute(value, axis, [(i, i ^ 1 << distance) for i in range(lax.axis...  15.3 us
    all_to_all x1, waiting for transfers between devices, on_device(): lax.all_to_all(grad_q.reshape(row_count, -1), 'head', split_axis=0, conca...  13.1 us
    all_to_all x1, waiting for transfers between devices, on_device(): lax.all_to_all(queries, 'head', split_axis=1, concat_axis=0, tiled=True)  5.81 us
    ppermute x12, waiting for transfers between devices, from_partner(): lax.ppermute(value, axis, [(i, i ^ 1 << distance) for i in range(lax.axis...  5.76 us
    dot_general x4, matrix products, block_grads(): jnp.einsum('nhgbk,nkhd->nbhgd', dscores, key_blk, preferred_element_type=...  4.84 us
    dot_general x4, matrix products, block_grads(): jnp.einsum('nhgbk,nbhgd->nkhd', dscores, query_blk, preferred_element_typ...  3.7 us
    all_to_all x1, starting transfers between devices, on_device(): lax.all_to_all(grad_q.reshape(row_count, -1), 'head', split_axis=0, conca...  3.52 us
    all_to_all x1, starting transfers between devices, on_device(): lax.all_to_all(queries, 'head', split_axis=1, concat_axis=0, tiled=True)  3.47 us
  transfers between devices with their start and end apart: 22, of which 9 were waited for; matrix products, arithmetic and copies ran while one was open for 21% of the time, Pallas kernels for 0%

profile of v1, /device:TPU:24, one launch (start us, length us, event | category | flops | bytes accessed | tf_op | source)
XLA Modules:
  0.0 104.8 jit_solution(14926386399862688204)
XLA Ops:
  0.6 1.3 %multiply_bitcast_fusion = f32[8,8,32,128]{3,1,2,0:T(8,128)S(1)} fusion(bf16[64,4096]{1,0:T(8,128)(2,1)} %param.9, bf16[64,4096]{1,0:T(8,128)(2,1)} %param.10), kind=kLoop, calls=%fused_computation.60 | loop fusion | flops 786432 | bytes 2097152
  2.0 0.2 copy.141
  2.2 0.3 reduce_sum.9
  2.6 0.7 reshape.272
  3.3 3.2 %all-to-all-start.3 = ((f32[4,1,512]{2,1,0:T(1,128)}), f32[4,1,512]{2,1,0:T(1,128)S(1)}, u32[]{:S(2)}, u32[]{:S(2)}) async-start(f32[4,1,512]{2,1,0:T(1,128)} %reshape.272), calls=%async_computation.3 | async-start | bytes 16384 | tf_op jit(solution)/shard_map/all_to_all | solution.py:83
  6.6 0.6 copy_bitcast_fusion.4
  7.2 3.1 %all-to-all-done.3 = f32[4,1,512]{2,1,0:T(1,128)S(1)} async-done(((f32[4,1,512]{2,1,0:T(1,128)}), f32[4,1,512]{2,1,0:T(1,128)S(1)}, u32[]{:S(2)}, u32[]{:S(2)}) %all-to-all-start.3) | async-done | bytes 8224 | tf_op jit(solution)/shard_map/all_to_all | solution.py:83
  10.4 3.3 %all-to-all-start.1 = ((bf16[64,4,128]{2,0,1:T(8,128)(2,1)}), bf16[64,4,128]{2,0,1:T(8,128)(2,1)S(1)}, u32[]{:S(2)}, u32[]{:S(2)}) async-start(bf16[64,4,128]{2,0,1:T(8,128)(2,1)} %copy_bitcast_fusion.4), calls=%async_computation.1 | async-start | bytes 131072 | tf_op jit(solution)/shard_map/all_to_all | solution.py:80
  13.7 0.8 copy.184
  14.5 3.2 %all-to-all-done.1 = bf16[64,4,128]{2,0,1:T(8,128)(2,1)S(1)} async-done(((bf16[64,4,128]{2,0,1:T(8,128)(2,1)}), bf16[64,4,128]{2,0,1:T(8,128)(2,1)S(1)}, u32[]{:S(2)}, u32[]{:S(2)}) %all-to-all-start.1) | async-done | bytes 65568 | tf_op jit(solution)/shard_map/all_to_all | solution.py:80
  17.7 3.5 %all-to-all-start = ((bf16[64,4,1024]{2,0,1:T(8,128)(2,1)}), bf16[64,4,1024]{2,0,1:T(8,128)(2,1)S(1)}, u32[]{:S(2)}, u32[]{:S(2)}) async-start(bf16[64,4,1024]{2,0,1:T(8,128)(2,1)} %bitcast.354), calls=%async_computation | async-start | bytes 1048576 | tf_op jit(solution)/shard_map/all_to_all | solution.py:78
  21.5 0.5 collective-permute-start
  22.0 1.6 %collective-permute-start.1 = (bf16[64,128]{1,0:T(8,128)(2,1)S(1)}, bf16[64,128]{1,0:T(8,128)(2,1)S(1)}, u32[]{:S(2)}, u32[]{:S(2)}) collective-permute-start(bf16[64,128]{1,0:T(8,128)(2,1)S(1)} %bitcast.397), channel_id=1, source_target_pairs={{0,2},{1,3},{2,0},{3,1},{4,6},{5,7},{6,4},{7,5},{8,10},{9,11},{10,... | collective-permute-start | bytes 49160 | tf_op jit(solution)/shard_map/ppermute | solution.py:32
  23.7 0.8 copy.183
  24.5 5.8 %all-to-all-done = bf16[64,4,1024]{2,0,1:T(8,128)(2,1)S(1)} async-done(((bf16[64,4,1024]{2,0,1:T(8,128)(2,1)}), bf16[64,4,1024]{2,0,1:T(8,128)(2,1)S(1)}, u32[]{:S(2)}, u32[]{:S(2)}) %all-to-all-start) | async-done | bytes 524320 | tf_op jit(solution)/shard_map/all_to_all | solution.py:78
  30.4 3.5 %all-to-all-start.2 = ((bf16[64,4,1024]{2,0,1:T(8,128)(2,1)}), bf16[64,4,1024]{2,0,1:T(8,128)(2,1)S(1)}, u32[]{:S(2)}, u32[]{:S(2)}) async-start(bf16[64,4,1024]{2,0,1:T(8,128)(2,1)} %bitcast.353), calls=%async_computation.2 | async-start | bytes 1048576 | tf_op jit(solution)/shard_map/all_to_all | solution.py:81
  33.9 0.5 broadcast.122
  34.4 0.7 reduce
  35.2 0.6 gather_fusion
  35.7 1.6 %collective-permute-start.3 = (bf16[1,256,1,128]{3,1,2,0:T(8,128)(2,1)S(1)}, bf16[1,256,1,128]{3,1,2,0:T(8,128)(2,1)S(1)}, u32[]{:S(2)}, u32[]{:S(2)}) collective-permute-start(bf16[1,256,1,128]{3,1,2,0:T(8,128)(2,1)S(1)} %bitcast.381), channel_id=1, source_target_pairs={{0,4},{4,0},{8,12},{12,8},{16,20},{20,16},{24,28},{28,24},{1,5},{5... | collective-permute-start | bytes 196616 | tf_op jit(solution)/shard_map/ppermute | solution.py:40
  37.4 0.3 collective-permute-start.7
  37.8 0.4 collective-permute-start.5
  38.2 2.6 %collective-permute-start.8 = (bf16[1,256,1,128]{3,1,2,0:T(8,128)(2,1)S(1)}, bf16[1,256,1,128]{3,1,2,0:T(8,128)(2,1)S(1)}, u32[]{:S(2)}, u32[]{:S(2)}) collective-permute-start(bf16[1,256,1,128]{3,1,2,0:T(8,128)(2,1)S(1)} %bitcast.387), channel_id=1, source_target_pairs={{0,16},{4,20},{8,24},{12,28},{16,0},{20,4},{24,8},{28,12},{1,17},{... | collective-permute-start | bytes 196616 | tf_op jit(solution)/shard_map/ppermute | solution.py:40
  40.8 1.6 %collective-permute-start.6 = (bf16[1,256,1,128]{3,1,2,0:T(8,128)(2,1)S(1)}, bf16[1,256,1,128]{3,1,2,0:T(8,128)(2,1)S(1)}, u32[]{:S(2)}, u32[]{:S(2)}) collective-permute-start(bf16[1,256,1,128]{3,1,2,0:T(8,128)(2,1)S(1)} %bitcast.388), channel_id=1, source_target_pairs={{0,8},{4,12},{8,0},{12,4},{16,24},{20,28},{24,16},{28,20},{1,9},{5... | collective-permute-start | bytes 196616 | tf_op jit(solution)/shard_map/ppermute | solution.py:40
  42.7 1.6 %collective-permute-start.4 = (bf16[1,256,1,128]{3,1,2,0:T(8,128)(2,1)S(1)}, bf16[1,256,1,128]{3,1,2,0:T(8,128)(2,1)S(1)}, u32[]{:S(2)}, u32[]{:S(2)}) collective-permute-start(bf16[1,256,1,128]{3,1,2,0:T(8,128)(2,1)S(1)} %bitcast.389), channel_id=1, source_target_pairs={{0,4},{4,0},{8,12},{12,8},{16,20},{20,16},{24,28},{28,24},{1,5},{5... | collective-permute-start | bytes 196616 | tf_op jit(solution)/shard_map/ppermute | solution.py:40
  44.3 0.4 fusion.69
  44.8 0.6 convolution_bitcast_fusion.2
  45.3 1.7 %collective-permute-done.4 = bf16[1,256,1,128]{3,1,2,0:T(8,128)(2,1)S(1)} collective-permute-done((bf16[1,256,1,128]{3,1,2,0:T(8,128)(2,1)S(1)}, bf16[1,256,1,128]{3,1,2,0:T(8,128)(2,1)S(1)}, u32[]{:S(2)}, u32[]{:S(2)}) %collective-permute-start.4) | collective-permute-done | bytes 65568 | tf_op jit(solution)/shard_map/ppermute | solution.py:40
  47.1 0.6 fusion.17
  47.7 0.4 fusion.28
  48.1 1.6 %collective-permute-start.9 = (f32[1,256,1,128]{3,1,2,0:T(8,128)S(1)}, f32[1,256,1,128]{3,1,2,0:T(8,128)S(1)}, u32[]{:S(2)}, u32[]{:S(2)}) collective-permute-start(f32[1,256,1,128]{3,1,2,0:T(8,128)S(1)} %fusion.28), channel_id=1, source_target_pairs={{0,4},{4,0},{8,12},{12,8},{16,20},{20,16},{24,28},{28,24},{1,5},{5... | collective-permute-start | bytes 393224 | tf_op jit(solution)/shard_map/ppermute | solution.py:40
  49.7 0.4 fusion.67
  50.2 0.6 fusion.18
  50.8 1.1 %fusion.26 = f32[1,256,1,128]{3,1,2,0:T(8,128)} fusion(bf16[8,256,256]{1,2,0:T(8,128)(2,1)S(1)} %fusion.18, bf16[256,8,128]{2,1,0:T(8,128)(2,1)S(1)} %bitcast.370), kind=kOutput, calls=%fused_computation.43 | convolution fusion | flops 134250496 | bytes 1703936 | tf_op jit(solution)/shard_map/nhgbk,nbhgd->nkhd/dot_general | solution.py:63
  51.9 0.5 collective-permute-start.10
  52.3 0.4 fusion.71
  52.8 0.6 fusion.16
  53.4 0.3 fusion.88
  53.7 0.6 convolution_bitcast_fusion.1
  54.3 0.6 collective-permute-start.12
  54.9 1.6 %collective-permute-start.13 = (f32[1,256,1,128]{3,1,2,0:T(8,128)S(1)}, f32[1,256,1,128]{3,1,2,0:T(8,128)S(1)}, u32[]{:S(2)}, u32[]{:S(2)}) collective-permute-start(f32[1,256,1,128]{3,1,2,0:T(8,128)S(1)} %convolution_bitcast_fusion.1), channel_id=1, source_target_pairs={{0,8},{4,12},{8,0},{12,4},{16,24},{20,28},{24,16},{28,20},{1,9},{5... | collective-permute-start | bytes 393224 | tf_op jit(solution)/shard_map/ppermute | solution.py:40
  56.4 0.4 fusion.65
  56.9 0.6 convolution_bitcast_fusion
  57.4 0.4 collective-permute-start.14
  57.8 0.6 fusion.19
  58.4 1.3 %fusion.75 = f32[128,8,256]{2,0,1:T(8,128)} fusion(bf16[8,256,256]{1,2,0:T(8,128)(2,1)S(1)} %fusion.19, bf16[1,256,1,128]{3,1,2,0:T(8,128)(2,1)S(1)} %collective-permute-done.7), kind=kOutput, calls=%fused_computation.97 | convolution fusion | flops 134217728 | bytes 2162688 | tf_op jit(solution)/shard_map/nhgbk,nkhd->nbhgd/dot_general | solution.py:59
  59.7 1.3 %convolution_add_fusion.1 = f32[128,8,256]{2,0,1:T(8,128)} fusion(f32[128,8,256]{2,0,1:T(8,128)S(1)} %fusion.88, bf16[8,256,256]{1,2,0:T(8,128)(2,1)S(1)} %fusion.17, bf16[1,256,1,128]{3,1,2,0:T(8,128)(2,1)S(1)} %collective-permute-done.3), kind=kOutput, calls=%fused_computation.31 | convolution fusion | flops 134479872 | bytes 3211264 | tf_op jit(solution)/shard_map/nhgbk,nkhd->nbhgd/dot_general | solution.py:59
  61.1 1.1 %fusion.24 = f32[1,256,1,128]{3,1,2,0:T(8,128)} fusion(bf16[8,256,256]{1,2,0:T(8,128)(2,1)S(1)} %fusion.19, bf16[256,8,128]{2,1,0:T(8,128)(2,1)S(1)} %bitcast.373), kind=kOutput, calls=%fused_computation.40 | convolution fusion | flops 134250496 | bytes 1703936 | tf_op jit(solution)/shard_map/nhgbk,nbhgd->nkhd/dot_general | solution.py:63
  62.2 2.6 %collective-permute-start.11 = (f32[1,256,1,128]{3,1,2,0:T(8,128)}, f32[1,256,1,128]{3,1,2,0:T(8,128)S(1)}, u32[]{:S(2)}, u32[]{:S(2)}) collective-permute-start(f32[1,256,1,128]{3,1,2,0:T(8,128)} %fusion.24), channel_id=1, source_target_pairs={{0,16},{4,20},{8,24},{12,28},{16,0},{20,4},{24,8},{28,12},{1,17},{... | collective-permute-start | bytes 393224 | tf_op jit(solution)/shard_map/ppermute | solution.py:40
  64.8 4.0 %collective-permute-done.14 = f32[1,256,1,128]{3,1,2,0:T(8,128)S(1)} collective-permute-done((f32[1,256,1,128]{3,1,2,0:T(8,128)S(1)}, f32[1,256,1,128]{3,1,2,0:T(8,128)S(1)}, u32[]{:S(2)}, u32[]{:S(2)}) %collective-permute-start.14) | collective-permute-done | bytes 131104 | tf_op jit(solution)/shard_map/ppermute | solution.py:40
  68.8 1.2 %fusion.36 = f32[1,256,1,128]{3,1,2,0:T(8,128)} fusion(f32[1,256,1,128]{3,1,2,0:T(8,128)S(1)} %collective-permute-done.14, f32[1,256,1,128]{3,1,2,0:T(8,128)S(1)} %collective-permute-done.13, f32[1,256,1,128]{3,1,2,0:T(8,128)S(1)} %collective-permute-done.12, f32[256,256,8]{1,0,2:T(8,128)S(1)} %fusion.71, f32[8,256]{1,0:T(8,128)S(1)} %copy-done.2, ...), kind=kOutput, calls=%fused_computation.55 | convolution fusion | flops 135888896 | bytes 3153920 | tf_op jit(solution)/shard_map/nhgbk,nbhgd->nkhd/dot_general | solution.py:55
  70.0 3.3 %all-to-all-start.6 = ((f32[4,64,128]{2,1,0:T(8,128)}), f32[4,64,128]{2,1,0:T(8,128)S(1)}, u32[]{:S(2)}, u32[]{:S(2)}) async-start(f32[4,64,128]{2,1,0:T(8,128)} %bitcast.95), calls=%async_computation.6 | async-start | bytes 262144 | tf_op jit(solution)/shard_map/all_to_all | solution.py:112
  73.4 1.1 %fusion.33 = f32[1,256,1,128]{3,1,2,0:T(8,128)} fusion(f32[1,256,1,128]{3,1,2,0:T(8,128)S(1)} %collective-permute-done.11, f32[1,256,1,128]{3,1,2,0:T(8,128)S(1)} %collective-permute-done.10, f32[1,256,1,128]{3,1,2,0:T(8,128)S(1)} %collective-permute-done.9, bf16[8,256,256]{1,2,0:T(8,128)(2,1)S(1)} %fusion.16, bf16[256,8,128]{2,1,0:T(8,128)(2,1)S(1)} %bitcast.374), kind=kOutput, calls=%fused_computation.52 | convolution fusion | flops 134348800 | bytes 2097152 | tf_op jit(solution)/shard_map/nhgbk,nbhgd->nkhd/dot_general | solution.py:63
  74.5 3.4 %all-to-all-done.6 = f32[4,64,128]{2,1,0:T(8,128)S(1)} async-done(((f32[4,64,128]{2,1,0:T(8,128)}), f32[4,64,128]{2,1,0:T(8,128)S(1)}, u32[]{:S(2)}, u32[]{:S(2)}) %all-to-all-start.6) | async-done | bytes 131104 | tf_op jit(solution)/shard_map/all_to_all | solution.py:112
  77.9 3.3 %all-to-all-start.5 = ((f32[4,64,128]{2,1,0:T(8,128)}), f32[4,64,128]{2,1,0:T(8,128)S(1)}, u32[]{:S(2)}, u32[]{:S(2)}) async-start(f32[4,64,128]{2,1,0:T(8,128)} %bitcast.73), calls=%async_computation.5 | async-start | bytes 262144 | tf_op jit(solution)/shard_map/all_to_all | solution.py:109
  81.2 1.9 %fusion.22 = f32[1,256,1,8,128]{1,4,3,2,0:T(8,128)S(1)} fusion(f32[128,8,256]{2,0,1:T(8,128)} %fusion.75, f32[128,8,256]{2,0,1:T(8,128)} %convolution_add_fusion.1, bf16[8,256,256]{1,2,0:T(8,128)(2,1)S(1)} %fusion.18, bf16[1,256,1,128]{3,1,2,0:T(8,128)(2,1)S(1)} %collective-permute-done.5), kind=kOutput, calls=%fused_computation.33 | convolution fusion | flops 135004160 | bytes 4259840 | tf_op jit(solution)/shard_map/nhgbk,nkhd->nbhgd/dot_general | solution.py:59
  83.1 0.4 copy.105
  83.5 1.1 %all_to_all.102 = f32[4,64,1024]{2,1,0:T(8,128)} reshape(f32[1,256,1,8,128]{4,3,1,2,0:T(8,128)S(1)} %copy.105) | data formatting | bytes 2097152 | tf_op jit(solution)/shard_map/all_to_all | solution.py:106
  84.7 1.1 %all-to-all-done.5 = f32[4,64,128]{2,1,0:T(8,128)S(1)} async-done(((f32[4,64,128]{2,1,0:T(8,128)}), f32[4,64,128]{2,1,0:T(8,128)S(1)}, u32[]{:S(2)}, u32[]{:S(2)}) %all-to-all-start.5) | async-done | bytes 131104 | tf_op jit(solution)/shard_map/all_to_all | solution.py:109
  85.8 3.5 %all-to-all-start.4 = ((f32[4,64,1024]{2,1,0:T(8,128)}), f32[4,64,1024]{2,1,0:T(8,128)S(1)}, u32[]{:S(2)}, u32[]{:S(2)}) async-start(f32[4,64,1024]{2,1,0:T(8,128)} %all_to_all.102), calls=%async_computation.4 | async-start | bytes 2097152 | tf_op jit(solution)/shard_map/all_to_all | solution.py:106
  89.3 0.7 copy_bitcast_fusion.2
  90.0 0.7 copy_bitcast_fusion.3
  90.7 13.1 %all-to-all-done.4 = f32[4,64,1024]{2,1,0:T(8,128)S(1)} async-done(((f32[4,64,1024]{2,1,0:T(8,128)}), f32[4,64,1024]{2,1,0:T(8,128)S(1)}, u32[]{:S(2)}, u32[]{:S(2)}) %all-to-all-start.4) | async-done | bytes 1048608 | tf_op jit(solution)/shard_map/all_to_all | solution.py:106
  103.7 1.0 copy.136
  (42 shorter events, 0.9 us)
Async XLA Ops:
  0.6 6.0 %copy-start = (bf16[64,512]{1,0:T(8,128)(2,1)S(1)}, bf16[64,512]{1,0:T(8,128)(2,1)}, u32[]{:S(2)}) copy-start(bf16[64,512]{1,0:T(8,128)(2,1)} %param.8) | copy-start | bytes 196612
  2.0 11.7 %copy-start.3 = (bf16[64,4096]{1,0:T(8,128)(2,1)S(1)}, bf16[64,4096]{1,0:T(8,128)(2,1)}, u32[]{:S(2)}) copy-start(bf16[64,4096]{1,0:T(8,128)(2,1)} %param.6) | copy-start | bytes 1572868
  2.2 19.1 %copy-start.4 = (bf16[64,512]{1,0:T(8,128)(2,1)S(1)}, bf16[64,512]{1,0:T(8,128)(2,1)}, u32[]{:S(2)}) copy-start(bf16[64,512]{1,0:T(8,128)(2,1)} %param.7) | copy-start | bytes 196612
  2.2 21.5 %copy-start.1 = (bf16[64,4096]{1,0:T(8,128)(2,1)S(1)}, bf16[64,4096]{1,0:T(8,128)(2,1)}, u32[]{:S(2)}) copy-start(bf16[64,4096]{1,0:T(8,128)(2,1)} %param.10) | copy-start | bytes 1572868
  3.3 7.0 %all-to-all-start.3 = ((f32[4,1,512]{2,1,0:T(1,128)}), f32[4,1,512]{2,1,0:T(1,128)S(1)}, u32[]{:S(2)}, u32[]{:S(2)}) async-start(f32[4,1,512]{2,1,0:T(1,128)} %reshape.272), calls=%async_computation.3 | async-start | bytes 16384 | tf_op jit(solution)/shard_map/all_to_all | solution.py:83
  10.4 7.4 %all-to-all-start.1 = ((bf16[64,4,128]{2,0,1:T(8,128)(2,1)}), bf16[64,4,128]{2,0,1:T(8,128)(2,1)S(1)}, u32[]{:S(2)}, u32[]{:S(2)}) async-start(bf16[64,4,128]{2,0,1:T(8,128)(2,1)} %copy_bitcast_fusion.4), calls=%async_computation.1 | async-start | bytes 131072 | tf_op jit(solution)/shard_map/all_to_all | solution.py:80
  17.7 12.6 %all-to-all-start = ((bf16[64,4,1024]{2,0,1:T(8,128)(2,1)}), bf16[64,4,1024]{2,0,1:T(8,128)(2,1)S(1)}, u32[]{:S(2)}, u32[]{:S(2)}) async-start(bf16[64,4,1024]{2,0,1:T(8,128)(2,1)} %bitcast.354), calls=%async_computation | async-start | bytes 1048576 | tf_op jit(solution)/shard_map/all_to_all | solution.py:78
  21.5 13.7 %collective-permute-start = (bf16[64,128]{1,0:T(8,128)(2,1)S(1)}, bf16[64,128]{1,0:T(8,128)(2,1)S(1)}, u32[]{:S(2)}, u32[]{:S(2)}) collective-permute-start(bf16[64,128]{1,0:T(8,128)(2,1)S(1)} %bitcast.396), channel_id=1, source_target_pairs={{0,1},{1,0},{2,3},{3,2},{4,5},{5,4},{6,7},{7,6},{8,9},{9,8},{10,11... | collective-permute-start | bytes 49160 | tf_op jit(solution)/shard_map/ppermute | solution.py:32
  22.0 13.2 %collective-permute-start.1 = (bf16[64,128]{1,0:T(8,128)(2,1)S(1)}, bf16[64,128]{1,0:T(8,128)(2,1)S(1)}, u32[]{:S(2)}, u32[]{:S(2)}) collective-permute-start(bf16[64,128]{1,0:T(8,128)(2,1)S(1)} %bitcast.397), channel_id=1, source_target_pairs={{0,2},{1,3},{2,0},{3,1},{4,6},{5,7},{6,4},{7,5},{8,10},{9,11},{10,... | collective-permute-start | bytes 49160 | tf_op jit(solution)/shard_map/ppermute | solution.py:32
  23.6 11.5 %collective-permute-start.2 = (bf16[64,128]{1,0:T(8,128)(2,1)S(1)}, bf16[64,128]{1,0:T(8,128)(2,1)S(1)}, u32[]{:S(2)}, u32[]{:S(2)}) collective-permute-start(bf16[64,128]{1,0:T(8,128)(2,1)S(1)} %bitcast.398), channel_id=1, source_target_pairs={{0,3},{1,2},{2,1},{3,0},{4,7},{5,6},{6,5},{7,4},{8,11},{9,10},{10,... | collective-permute-start | bytes 49160 | tf_op jit(solution)/shard_map/ppermute | solution.py:32
  30.4 12.3 %all-to-all-start.2 = ((bf16[64,4,1024]{2,0,1:T(8,128)(2,1)}), bf16[64,4,1024]{2,0,1:T(8,128)(2,1)S(1)}, u32[]{:S(2)}, u32[]{:S(2)}) async-start(bf16[64,4,1024]{2,0,1:T(8,128)(2,1)} %bitcast.353), calls=%async_computation.2 | async-start | bytes 1048576 | tf_op jit(solution)/shard_map/all_to_all | solution.py:81
  35.7 7.0 %collective-permute-start.3 = (bf16[1,256,1,128]{3,1,2,0:T(8,128)(2,1)S(1)}, bf16[1,256,1,128]{3,1,2,0:T(8,128)(2,1)S(1)}, u32[]{:S(2)}, u32[]{:S(2)}) collective-permute-start(bf16[1,256,1,128]{3,1,2,0:T(8,128)(2,1)S(1)} %bitcast.381), channel_id=1, source_target_pairs={{0,4},{4,0},{8,12},{12,8},{16,20},{20,16},{24,28},{28,24},{1,5},{5... | collective-permute-start | bytes 196616 | tf_op jit(solution)/shard_map/ppermute | solution.py:40
  37.4 17.4 %collective-permute-start.7 = (bf16[1,256,1,128]{3,1,2,0:T(8,128)(2,1)S(1)}, bf16[1,256,1,128]{3,1,2,0:T(8,128)(2,1)S(1)}, u32[]{:S(2)}, u32[]{:S(2)}) collective-permute-start(bf16[1,256,1,128]{3,1,2,0:T(8,128)(2,1)S(1)} %bitcast.382), channel_id=1, source_target_pairs={{0,16},{4,20},{8,24},{12,28},{16,0},{20,4},{24,8},{28,12},{1,17},{... | collective-permute-start | bytes 196616 | tf_op jit(solution)/shard_map/ppermute | solution.py:40
  37.8 11.9 %collective-permute-start.5 = (bf16[1,256,1,128]{3,1,2,0:T(8,128)(2,1)S(1)}, bf16[1,256,1,128]{3,1,2,0:T(8,128)(2,1)S(1)}, u32[]{:S(2)}, u32[]{:S(2)}) collective-permute-start(bf16[1,256,1,128]{3,1,2,0:T(8,128)(2,1)S(1)} %bitcast.383), channel_id=1, source_target_pairs={{0,8},{4,12},{8,0},{12,4},{16,24},{20,28},{24,16},{28,20},{1,9},{5... | collective-permute-start | bytes 196616 | tf_op jit(solution)/shard_map/ppermute | solution.py:40
  38.2 19.2 %collective-permute-start.8 = (bf16[1,256,1,128]{3,1,2,0:T(8,128)(2,1)S(1)}, bf16[1,256,1,128]{3,1,2,0:T(8,128)(2,1)S(1)}, u32[]{:S(2)}, u32[]{:S(2)}) collective-permute-start(bf16[1,256,1,128]{3,1,2,0:T(8,128)(2,1)S(1)} %bitcast.387), channel_id=1, source_target_pairs={{0,16},{4,20},{8,24},{12,28},{16,0},{20,4},{24,8},{28,12},{1,17},{... | collective-permute-start | bytes 196616 | tf_op jit(solution)/shard_map/ppermute | solution.py:40
  40.8 9.4 %collective-permute-start.6 = (bf16[1,256,1,128]{3,1,2,0:T(8,128)(2,1)S(1)}, bf16[1,256,1,128]{3,1,2,0:T(8,128)(2,1)S(1)}, u32[]{:S(2)}, u32[]{:S(2)}) collective-permute-start(bf16[1,256,1,128]{3,1,2,0:T(8,128)(2,1)S(1)} %bitcast.388), channel_id=1, source_target_pairs={{0,8},{4,12},{8,0},{12,4},{16,24},{20,28},{24,16},{28,20},{1,9},{5... | collective-permute-start | bytes 196616 | tf_op jit(solution)/shard_map/ppermute | solution.py:40
  42.5 2.3 %copy-start.2 = (f32[8,256]{1,0:T(8,128)S(1)}, f32[8,256]{1,0:T(8,128)}, u32[]{:S(2)}) copy-start(f32[8,256]{1,0:T(8,128)} %param.11) | copy-start | bytes 24580
  42.7 4.3 %collective-permute-start.4 = (bf16[1,256,1,128]{3,1,2,0:T(8,128)(2,1)S(1)}, bf16[1,256,1,128]{3,1,2,0:T(8,128)(2,1)S(1)}, u32[]{:S(2)}, u32[]{:S(2)}) collective-permute-start(bf16[1,256,1,128]{3,1,2,0:T(8,128)(2,1)S(1)} %bitcast.389), channel_id=1, source_target_pairs={{0,4},{4,0},{8,12},{12,8},{16,20},{20,16},{24,28},{28,24},{1,5},{5... | collective-permute-start | bytes 196616 | tf_op jit(solution)/shard_map/ppermute | solution.py:40
  48.1 25.2 %collective-permute-start.9 = (f32[1,256,1,128]{3,1,2,0:T(8,128)S(1)}, f32[1,256,1,128]{3,1,2,0:T(8,128)S(1)}, u32[]{:S(2)}, u32[]{:S(2)}) collective-permute-start(f32[1,256,1,128]{3,1,2,0:T(8,128)S(1)} %fusion.28), channel_id=1, source_target_pairs={{0,4},{4,0},{8,12},{12,8},{16,20},{20,16},{24,28},{28,24},{1,5},{5... | collective-permute-start | bytes 393224 | tf_op jit(solution)/shard_map/ppermute | solution.py:40
  51.9 21.5 %collective-permute-start.10 = (f32[1,256,1,128]{3,1,2,0:T(8,128)}, f32[1,256,1,128]{3,1,2,0:T(8,128)S(1)}, u32[]{:S(2)}, u32[]{:S(2)}) collective-permute-start(f32[1,256,1,128]{3,1,2,0:T(8,128)} %fusion.26), channel_id=1, source_target_pairs={{0,8},{4,12},{8,0},{12,4},{16,24},{20,28},{24,16},{28,20},{1,9},{5... | collective-permute-start | bytes 393224 | tf_op jit(solution)/shard_map/ppermute | solution.py:40
  54.3 7.9 %collective-permute-start.12 = (f32[1,256,1,128]{3,1,2,0:T(8,128)S(1)}, f32[1,256,1,128]{3,1,2,0:T(8,128)S(1)}, u32[]{:S(2)}, u32[]{:S(2)}) collective-permute-start(f32[1,256,1,128]{3,1,2,0:T(8,128)S(1)} %convolution_bitcast_fusion.2), channel_id=1, source_target_pairs={{0,4},{4,0},{8,12},{12,8},{16,20},{20,16},{24,28},{28,24},{1,5},{5... | collective-permute-start | bytes 393224 | tf_op jit(solution)/shard_map/ppermute | solution.py:40
  54.9 9.9 %collective-permute-start.13 = (f32[1,256,1,128]{3,1,2,0:T(8,128)S(1)}, f32[1,256,1,128]{3,1,2,0:T(8,128)S(1)}, u32[]{:S(2)}, u32[]{:S(2)}) collective-permute-start(f32[1,256,1,128]{3,1,2,0:T(8,128)S(1)} %convolution_bitcast_fusion.1), channel_id=1, source_target_pairs={{0,8},{4,12},{8,0},{12,4},{16,24},{20,28},{24,16},{28,20},{1,9},{5... | collective-permute-start | bytes 393224 | tf_op jit(solution)/shard_map/ppermute | solution.py:40
  57.4 11.3 %collective-permute-start.14 = (f32[1,256,1,128]{3,1,2,0:T(8,128)S(1)}, f32[1,256,1,128]{3,1,2,0:T(8,128)S(1)}, u32[]{:S(2)}, u32[]{:S(2)}) collective-permute-start(f32[1,256,1,128]{3,1,2,0:T(8,128)S(1)} %convolution_bitcast_fusion), channel_id=1, source_target_pairs={{0,16},{4,20},{8,24},{12,28},{16,0},{20,4},{24,8},{28,12},{1,17},{... | collective-permute-start | bytes 393224 | tf_op jit(solution)/shard_map/ppermute | solution.py:40
  62.2 11.2 %collective-permute-start.11 = (f32[1,256,1,128]{3,1,2,0:T(8,128)}, f32[1,256,1,128]{3,1,2,0:T(8,128)S(1)}, u32[]{:S(2)}, u32[]{:S(2)}) collective-permute-start(f32[1,256,1,128]{3,1,2,0:T(8,128)} %fusion.24), channel_id=1, source_target_pairs={{0,16},{4,20},{8,24},{12,28},{16,0},{20,4},{24,8},{28,12},{1,17},{... | collective-permute-start | bytes 393224 | tf_op jit(solution)/shard_map/ppermute | solution.py:40
  70.0 7.9 %all-to-all-start.6 = ((f32[4,64,128]{2,1,0:T(8,128)}), f32[4,64,128]{2,1,0:T(8,128)S(1)}, u32[]{:S(2)}, u32[]{:S(2)}) async-start(f32[4,64,128]{2,1,0:T(8,128)} %bitcast.95), calls=%async_computation.6 | async-start | bytes 262144 | tf_op jit(solution)/shard_map/all_to_all | solution.py:112
  77.9 7.9 %all-to-all-start.5 = ((f32[4,64,128]{2,1,0:T(8,128)}), f32[4,64,128]{2,1,0:T(8,128)S(1)}, u32[]{:S(2)}, u32[]{:S(2)}) async-start(f32[4,64,128]{2,1,0:T(8,128)} %bitcast.73), calls=%async_computation.5 | async-start | bytes 262144 | tf_op jit(solution)/shard_map/all_to_all | solution.py:109
  85.8 17.9 %all-to-all-start.4 = ((f32[4,64,1024]{2,1,0:T(8,128)}), f32[4,64,1024]{2,1,0:T(8,128)S(1)}, u32[]{:S(2)}, u32[]{:S(2)}) async-start(f32[4,64,1024]{2,1,0:T(8,128)} %all_to_all.102), calls=%async_computation.4 | async-start | bytes 2097152 | tf_op jit(solution)/shard_map/all_to_all | solution.py:106
